TPU v7x, 32 devices: a whole 2x2x4 slice. The times are simulated.
32 devices in a mesh: img: 4 (over y, core), bank: 8 (over z, x).
Axes of the slice: x: 2, y: 2, z: 4, core: 2. Of those that a mesh axis runs over, the one named last changes fastest.
Arguments:
- boxes: bfloat16 [8, 256, 768], P('img'), may hold values from -80 to 80
- prototypes: bfloat16 [65536, 768], P('bank'), may hold values from -3 to 3
- counts: int32 [4, 2], P('img'), may hold values from 1 to 256, 320 in all within a row
- keep: int32 [8, 256], P('img'), may hold values 0 or 1
Outputs:
- targets: bfloat16 [8, 256, 768], P('img', 'bank')
- top_logprob: float32 [8, 256], P('img', 'bank')
- log_norm: float32 [8, 256], P('img', 'bank')
Inputs may be any that keep to these rules, and one draw needn't show every extreme that they name: The counts of each group of 2 images sum to exactly 320.
All inputs are finite; a program needn't handle non-finite values. No bound on the sum of `keep` on one device may be relied on, other than what follows from the above.
Results may differ from a plain program's by a relative error of at most 0.0025.
Values sent between devices are 32-bit elements; how exact they have to be, the bound alone decides.
No kernel may reach another device: no remote copies, remote signals or barrier semaphores. Data moves between devices by JAX's collectives and lax.ppermute only.
A program may use at most 128 MiB of HBM per device.

v0:
```python
import functools

import jax
import jax.numpy as jnp
from jax import lax
from jax.experimental import pallas as pl
from jax.experimental.pallas import tpu as pltpu
from jax.sharding import PartitionSpec as P


LIVE = 320
F32 = jnp.float32
BF16 = jnp.bfloat16
TILE = 2048
PIECE = 512


class Plan:
    def __init__(self, boxes, banks):
        self.boxes, self.banks = boxes, banks
        self.share = boxes // banks
        self.half = LIVE // 2
        self.base = LIVE - boxes
        self.flex = boxes - self.half
        self.near = 4
        self.far = banks // self.near
        self.long_blocks = self.half // self.share
        self.base_blocks = self.base // self.share
        self.short_far = -(-self.long_blocks // self.near)
        self.short_half = [sum(self.half_owner(b, i, 0) < self.long_blocks for i in range(banks // 2))
                           for b in (0, 1)]

    def half_owner(self, bit, i, value):
        if bit == 0:
            return 2 * i + value
        return i // 2 * 4 + 2 * value + i % 2

    def half_index(self, bit, owner):
        return owner // 2 if bit == 0 else owner // 4 * 2 + owner % 2

    def half_rows(self, bit):
        return self.share * (self.banks // 2 + self.short_half[bit])

    def half_blocks(self, bit, value):
        own = [self.half_owner(bit, i, value) for i in range(self.banks // 2)]
        return [self.share * o for o in own] + [self.short_row(o) for o in own[:self.short_half[bit]]]

    def quarter_rows(self):
        return self.share * (self.far + self.short_far)

    def quarter_picks(self, bit, me):
        lists = []
        for low in (me % 4, me % 4 ^ (2 >> bit)):
            picks = []
            for h in range(self.far):
                owner = self.near * h + low
                picks.append((self.half_index(bit, owner), self.share * owner))
            for h in range(self.short_far):
                owner = self.near * h + low
                q = jnp.minimum(self.half_index(bit, owner), self.short_half[bit] - 1)
                picks.append((self.banks // 2 + q, self.short_row(owner)))
            lists.append(picks)
        return lists

    def own_picks(self, me):
        lists = []
        for s in range(self.far):
            to = me // 4 ^ s
            owner = self.near * to + me % 4
            q = self.far + jnp.minimum(to, self.short_far - 1)
            lists.append([(to, self.share * owner), (q, self.short_row(owner))])
        return lists

    def short_row(self, owner):
        owner = jnp.minimum(owner, self.long_blocks - 1)
        return jnp.where(
            owner < self.base_blocks,
            self.boxes + self.share * owner,
            self.half + self.share * (self.long_blocks - 1 - owner),
        )


def iota(shape, axis):
    return lax.broadcasted_iota(jnp.int32, shape, axis)


def long_image(cnt_ref):
    return jnp.where(cnt_ref[0, 1] > cnt_ref[0, 0], 1, 0)


def bank_kernel(plan, cols, firsts, carry, cnt_ref, pos_ref, boxes_hbm, bank_hbm, *rest):
    stat_ref = rest[0]
    chunks = len(firsts)
    outs = rest[1:1 + 2 * chunks]
    boxes_ref, x_v, bank_v, s_v, acc_v, box_sem, sems = rest[1 + 2 * chunks:]
    box_copy = pltpu.make_async_copy(boxes_hbm, boxes_ref, box_sem)
    box_copy.start()
    bank = bank_v.shape[0]
    tile = min(TILE, bank)

    def piece(i):
        rows = pl.ds(i * PIECE, PIECE)
        return pltpu.make_async_copy(bank_hbm.at[rows], bank_v.at[rows], sems.at[i])

    per = tile // PIECE
    for i in range(per):
        piece(i).start()
    box_copy.wait()
    half, base, boxes, flex = plan.half, plan.base, plan.boxes, plan.flex
    li = long_image(cnt_ref)
    si = 1 - li
    extra = cnt_ref[0, li] - half
    flip = (iota((flex, flex), 0) + iota((flex, flex), 1) == flex - 1).astype(BF16)
    back = jnp.dot(flip, boxes_ref[si, base:half, :], preferred_element_type=F32)
    front = boxes_ref[li, half:boxes, :].astype(F32)
    x_v[0:half, :] = boxes_ref[li, 0:half, :]
    x_v[half:boxes, :] = jnp.where(iota(front.shape, 0) < extra, front, back).astype(BF16)
    x_v[boxes:LIVE, :] = boxes_ref[si, 0:base, :]
    for i in range(per, min(2 * per, bank // PIECE)):
        piece(i).start()

    def scores(i, top):
        for k in range(per):
            piece(i * per + k).wait()

        @pl.when(i + 2 < bank // tile)
        def _():
            for k in range(per):
                piece((i + 2) * per + k).start()

        s = lax.dot_general(x_v[...], bank_v[pl.ds(i * tile, tile)], (((1,), (1,)), ((), ())),
                            preferred_element_type=F32)
        s_v[i] = s
        for j in range(tile // 128):
            top = jnp.maximum(top, s[:, j * 128:(j + 1) * 128])
        return top

    top = lax.fori_loop(0, bank // tile, scores, jnp.full((LIVE, 128), -jnp.inf, F32))
    peak = jnp.max(top, axis=1, keepdims=True)
    acc_v[...] = jnp.zeros_like(acc_v)

    def pulls(i, mass):
        e = jnp.exp(s_v[i] - peak)
        for j in range(tile // 128):
            mass = mass + e[:, j * 128:(j + 1) * 128]
        acc_v[...] += jnp.dot(e.astype(BF16), bank_v[pl.ds(i * tile, tile)],
                              preferred_element_type=F32)
        return mass

    mass = lax.fori_loop(0, bank // tile, pulls, jnp.zeros((LIVE, 128), F32))
    mass = jnp.sum(mass, axis=1, keepdims=True)
    both = jnp.where(iota((LIVE, 128), 1) == 0, peak, mass)
    lanes = jnp.transpose(both)[0:8, :]
    pad = jnp.zeros((1, 2 * boxes - LIVE), F32)
    packed = jnp.concatenate([
        lanes[0:1, 0:boxes],
        jnp.concatenate([lanes[0:1, boxes:LIVE], pad], axis=1),
        lanes[1:2, 0:boxes],
        jnp.concatenate([lanes[1:2, boxes:LIVE], pad], axis=1),
        jnp.zeros((4, boxes), F32)], axis=0)
    stat_ref[...] = packed
    share = plan.share
    for c, bit in enumerate(firsts):
        mine = pos_ref[0] // (1 << bit) % 2
        if carry[c]:
            rows = plan.half_rows(bit)
            outs[2 * c + 1][rows:rows + 8, :] = packed
        for kind, value in ((0, mine), (1, 1 - mine)):
            for q, row in enumerate(plan.half_blocks(bit, value)):
                outs[2 * c + kind][q * share:(q + 1) * share, :] = acc_v[
                    pl.ds(pl.multiple_of(row, 8), share), c * cols:(c + 1) * cols]


def merge_stats(tiles):
    peak = functools.reduce(jnp.maximum, [t[0:2, :] for t in tiles])
    factors = [jnp.exp(t[0:2, :] - peak) for t in tiles]
    mass = functools.reduce(jnp.add, [t[2:4, :] * f for t, f in zip(tiles, factors)])
    return peak, factors, mass


def store_columns(plan, values, col_ref):
    width = plan.boxes
    fill = [jnp.zeros((1, width), F32)] * (8 - len(values))
    top = jnp.transpose(jnp.concatenate([v[0:1, :] for v in values] + fill, axis=0))
    low = jnp.transpose(jnp.concatenate([v[1:2, :] for v in values] + fill, axis=0))
    col_ref[0:width, :] = top
    col_ref[width:LIVE, :] = low[0:LIVE - width, :]


def merge_kernel(plan, picks, has_tile, pos_ref, own_ref, got_ref, mine_ref, theirs_ref, *rest):
    outs, col_v = rest[:-1], rest[-1]
    share = plan.share
    peak, factors, mass = merge_stats([mine_ref[...], theirs_ref[...]])
    store_columns(plan, factors, col_v)
    for out_ref, blocks in zip(outs, picks(pos_ref[0])):
        for at, (q, row) in enumerate(blocks):
            src = pl.ds(pl.multiple_of(q * share, 8), share)
            col = col_v[pl.ds(pl.multiple_of(row, 8), share), :]
            out_ref[at * share:(at + 1) * share, :] = (
                own_ref[src, :] * col[:, 0:1] + got_ref[src, :] * col[:, 1:2])
        if has_tile:
            end = len(blocks) * share
            out_ref[end:end + 8, :] = jnp.concatenate([peak, mass, peak, mass], axis=0)


def conf_kernel(plan, cnt_ref, keep_ref, *refs):
    out_ref = refs[-1]
    base, boxes = plan.base, plan.boxes
    li = long_image(cnt_ref)
    keep_l = (keep_ref[pl.ds(li, 1), :] == 1).astype(F32)
    keep_s = (keep_ref[pl.ds(1 - li, 1), :] == 1).astype(F32)
    turn = (iota((boxes, boxes), 0) + iota((boxes, boxes), 1) == LIVE - 1).astype(BF16)
    turned = jnp.dot(jnp.broadcast_to(keep_s, (8, boxes)).astype(BF16), turn,
                     preferred_element_type=F32)[0:1, :]
    lane = iota((1, boxes), 1)
    live = jnp.concatenate([jnp.where(lane < cnt_ref[0, li], keep_l, turned),
                            jnp.where(lane < base, keep_s, 0.0)], axis=0)
    _, _, mass = merge_stats([r[...] for r in refs[:-1]])
    row = jnp.where(live > 0.5, -jnp.log(jnp.where(live > 0.5, mass, 1.0)), 0.0)
    total, count = jnp.sum(row), jnp.sum(live)
    out_ref[...] = jnp.where(iota((8, 128), 0) == 0, total, count)


def prep_kernel(plan, cnt_ref, pos_ref, keep_ref, *refs):
    far, share = plan.far, plan.share
    col_ref, neg_ref, norm_ref, col_v = refs[far:]
    me = pos_ref[0]
    li = long_image(cnt_ref)
    si = 1 - li
    peak, factors, mass = merge_stats([r[...] for r in refs[:far]])
    lane = iota((plan.boxes, 128), 1)
    src = iota((plan.boxes, 128), 0)
    slot = share * me + lane
    is_base = me < plan.base_blocks
    long_pick = (src == slot).astype(F32)
    short_pick = (src == jnp.where(is_base, slot, LIVE - 1 - slot)).astype(F32)
    keep = (keep_ref[...] == 1).astype(F32)
    stack = jnp.concatenate([peak, jnp.log(jnp.where(mass > 0.0, mass, 1.0)), mass, keep], axis=0)
    pick = functools.partial(jnp.dot, preferred_element_type=F32, precision=lax.Precision.HIGHEST)
    long_vals = pick(stack, long_pick)
    short_vals = pick(stack, short_pick)
    short_vals = jnp.where(is_base, pltpu.roll(short_vals, 7, 0), short_vals)
    slot_row = share * me + iota((1, 128), 1)
    live_rows = []
    for image, vals in ((li, long_vals), (si, short_vals)):
        kept = jnp.where(image == 0, long_vals[6:7, :], long_vals[7:8, :])
        live = (kept > 0.5) & (slot_row < cnt_ref[0, image])
        live_rows.append(live.astype(F32))
        norm = jnp.where(live, vals[0:1, :] + vals[2:3, :], 0.0)
        norm_ref[pl.ds(image, 1), :] = norm[:, 0:share]
        neg_ref[pl.ds(image, 1), :] = -vals[2:3, :]
        neg_ref[pl.ds(2 + image, 1), :] = live.astype(F32)
    live_cols = jnp.transpose(jnp.concatenate(live_rows + [jnp.zeros((6, 128), F32)], axis=0))
    weights = [f / jnp.where(mass > 0.0, mass, 1.0) for f in factors]
    for part in range(0, far, 6):
        store_columns(plan, weights[part:part + 6], col_v.at[part // 6])
    place = iota((share, 128), 1)
    for which, row in ((0, share * me), (1, plan.short_row(me))):
        out = jnp.where(place == far, live_cols[0:share, which:which + 1], 0.0)
        for s in range(far):
            col = col_v[s // 6, pl.ds(pl.multiple_of(row, 8), share), :]
            out = jnp.where(place == s, col[:, s % 6:s % 6 + 1], out)
        col_ref[which * share:(which + 1) * share, :] = out


def final_kernel(plan, chunks, images, cnt_ref, pos_ref, col_ref, neg_ref, *refs):
    far, share = plan.far, plan.share
    confs = refs[:images]
    pulls = refs[images:images + far * chunks]
    out_ref, prob_ref = refs[images + far * chunks:]
    me = pos_ref[0]
    li = long_image(cnt_ref)
    conf = functools.reduce(jnp.add, [c[...] for c in confs])
    mean = conf[0:1, 0:1] / jnp.maximum(conf[1:2, 0:1], 1.0)
    prob = jnp.where(neg_ref[2:4, :] > 0.5, neg_ref[0:2, :] - mean, 0.0)
    prob_ref[...] = prob[:, 0:share]
    width = pulls[0].shape[1]
    turned = (me >= plan.base_blocks) & (me < plan.long_blocks)
    a, b = iota((share, share), 0), iota((share, share), 1)
    order = (b == jnp.where(turned, share - 1 - a, a)).astype(BF16)
    for which, image in ((0, li), (1, 1 - li)):
        at = which * share
        col = col_ref[at:at + share, :]
        live = col[:, far:far + 1] > 0.5
        for c in range(chunks):
            value = functools.reduce(
                jnp.add, [pulls[c * far + s][at:at + share, :] * col[:, s:s + 1] for s in range(far)])
            value = value.astype(BF16)
            if which == 1:
                value = jnp.dot(order, value, preferred_element_type=F32).astype(BF16)
            out_ref[image, :, c * width:(c + 1) * width] = jnp.where(live, value, jnp.zeros_like(value))


VM = pl.BlockSpec(memory_space=pltpu.VMEM)
SM = pl.BlockSpec(memory_space=pltpu.SMEM)
HBM = pl.BlockSpec(memory_space=pltpu.HBM)
MIB = 2**20
VMEM_MIB = 52
FIRST_BIT = (0, 1, 0)


def call(body, ins, outs, scratch, flops, moved, limit, out_specs=None):
    return pl.pallas_call(
        body,
        out_shape=[jax.ShapeDtypeStruct(shape, dtype) for shape, dtype in outs],
        in_specs=ins,
        out_specs=out_specs or [VM] * len(outs),
        scratch_shapes=scratch,
        compiler_params=pltpu.CompilerParams(vmem_limit_bytes=limit * MIB),
        cost_estimate=pl.CostEstimate(flops=flops, bytes_accessed=moved, transcendentals=0),
    )


def on_device(boxes, prototypes, counts, keep):
    images, slots, width = boxes.shape
    bank = prototypes.shape[0]
    banks = lax.axis_size("bank")
    groups = lax.axis_size("img")
    plan = Plan(slots, banks)
    near, far, share = plan.near, plan.far, plan.share
    pos = lax.axis_index("bank").reshape(1)
    cols = slots
    chunks = width // cols
    firsts = [FIRST_BIT[c % len(FIRST_BIT)] for c in range(chunks)]
    carry = [bit not in firsts[:c] for c, bit in enumerate(firsts)]
    shapes = [((8, slots), F32)]
    for c in range(chunks):
        rows = plan.half_rows(firsts[c])
        shapes += [((rows, cols), F32), ((rows + 8 * carry[c], cols), F32)]
    stat, *parts = call(
        functools.partial(bank_kernel, plan, cols, firsts, carry),
        [SM, SM, HBM, HBM],
        shapes,
        [pltpu.VMEM(boxes.shape, BF16), pltpu.VMEM((LIVE, width), BF16),
         pltpu.VMEM((bank, width), BF16), pltpu.VMEM((bank // TILE, LIVE, TILE), F32),
         pltpu.VMEM((LIVE, width), F32), pltpu.SemaphoreType.DMA,
         pltpu.SemaphoreType.DMA((bank // PIECE,))],
        4 * LIVE * bank * width, bank * width * 2, VMEM_MIB,
    )(counts, pos, boxes, prototypes)

    def swap(array, step):
        return lax.ppermute(array, "bank", [(i, i ^ step) for i in range(banks)])

    def merge(picks, number, rows, has_tile, *arrays):
        return call(
            functools.partial(merge_kernel, plan, picks, has_tile),
            [SM] + [VM] * 4, [((rows + 8 * has_tile, cols), F32)] * number,
            [pltpu.VMEM((LIVE, 8), F32)],
            number * rows * cols * 4, number * rows * cols * 16, 8,
        )(pos, *arrays)

    got = [swap(parts[2 * c + 1], 1 << firsts[c]) for c in range(chunks)]
    first_tile = {firsts[c]: got[c][plan.half_rows(firsts[c]):] for c in range(chunks) if carry[c]}
    quarters = plan.quarter_rows()
    second_tiles = {}
    second = []
    for c, bit in enumerate(firsts):
        own, send = merge(functools.partial(plan.quarter_picks, bit), 2, quarters, carry[c],
                          parts[2 * c], got[c], stat, first_tile[bit])
        second.append((own, swap(send, 2 >> bit)))
        if carry[c]:
            second_tiles[bit] = (own[quarters:], second[c][1][quarters:])
    pulls = []
    for c, bit in enumerate(firsts):
        own, seen = second[c]
        if c == chunks - 1 and c > 0:
            own, pulls[-1][0] = lax.optimization_barrier((own, pulls[-1][0]))
        outs = merge(plan.own_picks, far, 2 * share, c == 0, own, seen, *second_tiles[bit])
        pulls.append([outs[0]] + [swap(outs[s], near * s) for s in range(1, far)])
    tiles = [p[2 * share:] for p in pulls[0]]

    conf, = call(functools.partial(conf_kernel, plan), [SM, VM] + [VM] * far, [((8, 128), F32)], [],
                 slots * 8, slots * 64, 4)(counts, keep, *tiles)
    confs = [conf] + [lax.ppermute(conf, "img", [(i, i ^ s) for i in range(groups)])
                      for s in range(1, groups)]
    col, neg, log_norm = call(
        functools.partial(prep_kernel, plan), [SM, SM, VM] + [VM] * far,
        [((2 * share, 128), F32), ((8, 128), F32), ((images, share), F32)],
        [pltpu.VMEM(((far + 5) // 6, LIVE, 8), F32)],
        slots * 8, slots * 64, 4,
    )(counts, pos, keep, *tiles)
    targets, top_logprob = call(
        functools.partial(final_kernel, plan, chunks, groups),
        [SM, SM, VM, VM] + [VM] * (groups + far * chunks),
        [((images, share, width), BF16), ((images, share), F32)], [],
        far * share * width * 4, far * share * width * 8, 8,
    )(counts, pos, col, neg, *confs, *[p for group in pulls for p in group])
    return targets, top_logprob, log_norm


def solution(mesh):
    placed = (P("img", None, None), P("bank", None), P("img", None), P("img", None))
    return jax.shard_map(
        on_device,
        mesh=mesh,
        in_specs=placed,
        out_specs=(P("img", "bank", None), P("img", "bank"), P("img", "bank")),
        check_vma=False,
    )
```

profile of v0, /device:TPU:0, one launch (start us, length us, event | category | flops | bytes accessed | tf_op | source)
XLA Modules:
  0.0 46.4 jit_solution(1621501391087128048)
XLA Ops:
  0.6 0.6 %copy-done.1 = s32[1,2]{1,0:T(1,128)S(1)} copy-done((s32[1,2]{1,0:T(1,128)S(1)}, s32[1,2]{1,0:T(1,128)}, u32[]{:S(2)}) %copy-start.1) | copy-done | bytes 32
  1.3 13.5 %shard_map.67 = (f32[8,256]{1,0:T(8,128)S(1)}, f32[224,256]{1,0:T(8,128)S(1)}, f32[232,256]{1,0:T(8,128)S(1)}, f32[224,256]{1,0:T(8,128)S(1)}, f32[232,256]{1,0:...) custom-call(s32[1,2]{1,0:T(1,128)S(1)} %copy-done.1, s32[1]{0:T(128)} %bitcast.pos_ref, ...), custom_call_target="tpu_custom_call" | custom-call | flops 8053063680 | bytes 12582912 | tf_op jit(solution)/shard_map/pallas_call | solution.py:330
  14.8 3.0 %collective-permute-start = (f32[232,256]{1,0:T(8,128)S(1)}, f32[232,256]{1,0:T(8,128)S(1)}, u32[]{:S(2)}, u32[]{:S(2)}) collective-permute-start(f32[232,256]{1,0:T(8,128)S(1)} %get-tuple-element.30), channel_id=1, source_target_pairs={{0,1},{1,0},{2,3},{3,2},{4,5},{5,4},{6,7},{7,6},{8,9},{9,8},{10,11... | collective-permute-start | bytes 712712 | tf_op jit(solution)/shard_map/ppermute | solution.py:342
  17.8 1.6 %collective-permute-start.7 = (f32[232,256]{1,0:T(8,128)S(1)}, f32[232,256]{1,0:T(8,128)S(1)}, u32[]{:S(2)}, u32[]{:S(2)}) collective-permute-start(f32[232,256]{1,0:T(8,128)S(1)} %get-tuple-element.42), channel_id=1, source_target_pairs={{0,2},{1,3},{2,0},{3,1},{4,6},{5,7},{6,4},{7,5},{8,10},{9,11},{10,... | collective-permute-start | bytes 712712 | tf_op jit(solution)/shard_map/ppermute | solution.py:342
  19.4 0.5 %collective-permute-start.6 = (f32[224,256]{1,0:T(8,128)S(1)}, f32[224,256]{1,0:T(8,128)S(1)}, u32[]{:S(2)}, u32[]{:S(2)}) collective-permute-start(f32[224,256]{1,0:T(8,128)S(1)} %get-tuple-element.39), channel_id=1, source_target_pairs={{0,1},{1,0},{2,3},{3,2},{4,5},{5,4},{6,7},{7,6},{8,9},{9,8},{10,11... | collective-permute-start | bytes 688136 | tf_op jit(solution)/shard_map/ppermute | solution.py:342
  20.0 4.5 %collective-permute-done.got_ref = f32[232,256]{1,0:T(8,128)S(1)} collective-permute-done((f32[232,256]{1,0:T(8,128)S(1)}, f32[232,256]{1,0:T(8,128)S(1)}, u32[]{:S(2)}, u32[]{:S(2)}) %collective-permute-start) | collective-permute-done | bytes 237600 | tf_op jit(solution)/shard_map/ppermute | solution.py:342
  24.5 0.4 shard_map.68
  24.8 2.2 %collective-permute-start.1 = (f32[136,256]{1,0:T(8,128)S(1)}, f32[136,256]{1,0:T(8,128)S(1)}, u32[]{:S(2)}, u32[]{:S(2)}) collective-permute-start(f32[136,256]{1,0:T(8,128)S(1)} %get-tuple-element.33), channel_id=1, source_target_pairs={{0,2},{1,3},{2,0},{3,1},{4,6},{5,7},{6,4},{7,5},{8,10},{9,11},{10,... | collective-permute-start | bytes 417800 | tf_op jit(solution)/shard_map/ppermute | solution.py:342
  27.0 0.0 collective-permute-done.7.got_ref
  27.0 0.4 shard_map.73
  27.4 1.6 %collective-permute-start.8 = (f32[136,256]{1,0:T(8,128)S(1)}, f32[136,256]{1,0:T(8,128)S(1)}, u32[]{:S(2)}, u32[]{:S(2)}) collective-permute-start(f32[136,256]{1,0:T(8,128)S(1)} %get-tuple-element.44), channel_id=1, source_target_pairs={{0,1},{1,0},{2,3},{3,2},{4,5},{5,4},{6,7},{7,6},{8,9},{9,8},{10,11... | collective-permute-start | bytes 417800 | tf_op jit(solution)/shard_map/ppermute | solution.py:342
  28.9 0.5 %collective-permute-done.6.got_ref = f32[224,256]{1,0:T(8,128)S(1)} collective-permute-done((f32[224,256]{1,0:T(8,128)S(1)}, f32[224,256]{1,0:T(8,128)S(1)}, u32[]{:S(2)}, u32[]{:S(2)}) %collective-permute-start.6) | collective-permute-done | bytes 229408 | tf_op jit(solution)/shard_map/ppermute | solution.py:342
  29.4 0.3 shard_map.72
  29.7 2.2 %collective-permute-start.10 = (f32[128,256]{1,0:T(8,128)S(1)}, f32[128,256]{1,0:T(8,128)S(1)}, u32[]{:S(2)}, u32[]{:S(2)}) collective-permute-start(f32[128,256]{1,0:T(8,128)S(1)} %get-tuple-element.49), channel_id=1, source_target_pairs={{0,2},{1,3},{2,0},{3,1},{4,6},{5,7},{6,4},{7,5},{8,10},{9,11},{10,... | collective-permute-start | bytes 393224 | tf_op jit(solution)/shard_map/ppermute | solution.py:342
  31.9 0.0 collective-permute-done.1.got_ref
  31.9 0.3 shard_map.69
  32.2 2.7 %collective-permute-start.2 = (f32[72,256]{1,0:T(8,128)S(1)}, f32[72,256]{1,0:T(8,128)S(1)}, u32[]{:S(2)}, u32[]{:S(2)}) collective-permute-start(f32[72,256]{1,0:T(8,128)S(1)} %get-tuple-element.35), channel_id=1, source_target_pairs={{0,4},{1,5},{2,6},{3,7},{4,0},{5,1},{6,2},{7,3},{8,12},{9,13},{10,... | collective-permute-start | bytes 221192 | tf_op jit(solution)/shard_map/ppermute | solution.py:342
  34.9 0.3 shard_map.74
  35.2 0.4 collective-permute-done.10.got_ref
  35.6 0.3 shard_map.75
  35.9 2.9 %collective-permute-start.11 = (f32[64,256]{1,0:T(8,128)S(1)}, f32[64,256]{1,0:T(8,128)S(1)}, u32[]{:S(2)}, u32[]{:S(2)}) collective-permute-start(f32[64,256]{1,0:T(8,128)S(1)} %get-tuple-element.51), channel_id=1, source_target_pairs={{0,4},{1,5},{2,6},{3,7},{4,0},{5,1},{6,2},{7,3},{8,12},{9,13},{10,... | collective-permute-start | bytes 196616 | tf_op jit(solution)/shard_map/ppermute | solution.py:342
  38.7 0.1 collective-permute-start.9
  38.8 1.6 %collective-permute-done.2.refs_5_ = f32[72,256]{1,0:T(8,128)S(1)} collective-permute-done((f32[72,256]{1,0:T(8,128)S(1)}, f32[72,256]{1,0:T(8,128)S(1)}, u32[]{:S(2)}, u32[]{:S(2)}) %collective-permute-start.2) | collective-permute-done | bytes 73760 | tf_op jit(solution)/shard_map/ppermute | solution.py:342
  40.4 0.8 %shard_map.71.refs_0_ = f32[8,128]{1,0:T(8,128)S(1)} custom-call(s32[1,2]{1,0:T(1,128)S(1)} %copy-done.1, s32[2,256]{1,0:T(2,128)S(1)} %copy-done, f32[8,256]{1,0:T(8,128)S(1)} %slice.27.refs_0_, f32[8,256]{1,0:T(8,128)S(1)} %slice.34.refs_1_), custom_call_target="tpu_custom_call" | custom-call | flops 2048 | bytes 16384 | tf_op jit(solution)/shard_map/pallas_call | solution.py:372
  41.3 0.1 collective-permute-start.5
  41.4 1.6 %collective-permute-start.4 = (f32[8,128]{1,0:T(8,128)S(1)}, f32[8,128]{1,0:T(8,128)S(1)}, u32[]{:S(2)}, u32[]{:S(2)}) collective-permute-start(f32[8,128]{1,0:T(8,128)S(1)} %shard_map.71.refs_0_), channel_id=1, source_target_pairs={{0,16},{8,24},{16,0},{24,8},{1,17},{9,25},{17,1},{25,9},{2,18},{10... | collective-permute-start | bytes 12296 | tf_op jit(solution)/shard_map/ppermute | solution.py:374
  43.0 0.2 collective-permute-start.3
  43.2 1.4 %shard_map.70 = (f32[64,128]{1,0:T(8,128)S(1)}, f32[8,128]{1,0:T(8,128)S(1)}, f32[2,32]{1,0:T(2,128)}) custom-call(s32[1,2]{1,0:T(1,128)S(1)} %copy-done.1, s32[1]{0:T(128)} %bitcast.pos_ref, s32[2,256]{1,0:T(2,128)S(1)} %copy-done, f32[8,256]{1,0:T(8,128)S(1)} %slice.27.refs_0_, f32[8,256]{1,0:T(8,128)S(1)} %slice.34.refs_1_), custom_call_target="tpu_custom_call" | custom-call | flops 2048 | bytes 16384 | tf_op jit(solution)/shard_map/pallas_call | solution.py:376
  44.6 0.0 collective-permute-done.9.refs_7_
  44.6 0.0 collective-permute-done.5.refs_3_
  44.6 0.4 collective-permute-done.4.refs_2_
  45.0 1.4 %shard_map.76 = (bf16[2,32,768]{2,1,0:T(8,128)(2,1)}, f32[2,32]{1,0:T(2,128)}) custom-call(s32[1,2]{1,0:T(1,128)S(1)} %copy-done.1, s32[1]{0:T(128)} %bitcast.pos_ref, f32[64,128]{1,0:T(8,128)S(1)} %get-tuple-element.36.col_ref, f32[8,128]{1,0:T(8,128)S(1)} %get-tuple-element.37.neg_ref, f32[8,128]{1,0:T(8,128)S(1)} %shard_map.71.refs_0_, ...), custom_call_target="tpu_custom_call" | custom-call | flops 196608 | bytes 393216 | tf_op jit(solution)/shard_map/pallas_call | solution.py:382
  (14 shorter events, 0.0 us)
Async XLA Ops:
  0.6 0.7 %copy-start.1 = (s32[1,2]{1,0:T(1,128)S(1)}, s32[1,2]{1,0:T(1,128)}, u32[]{:S(2)}) copy-start(s32[1,2]{1,0:T(1,128)} %cnt_ref.7) | copy-start | bytes 28
  1.3 39.2 %copy-start = (s32[2,256]{1,0:T(2,128)S(1)}, s32[2,256]{1,0:T(2,128)}, u32[]{:S(2)}) copy-start(s32[2,256]{1,0:T(2,128)} %keep_ref.3) | copy-start | bytes 6148
  14.8 9.7 %collective-permute-start = (f32[232,256]{1,0:T(8,128)S(1)}, f32[232,256]{1,0:T(8,128)S(1)}, u32[]{:S(2)}, u32[]{:S(2)}) collective-permute-start(f32[232,256]{1,0:T(8,128)S(1)} %get-tuple-element.30), channel_id=1, source_target_pairs={{0,1},{1,0},{2,3},{3,2},{4,5},{5,4},{6,7},{7,6},{8,9},{9,8},{10,11... | collective-permute-start | bytes 712712 | tf_op jit(solution)/shard_map/ppermute | solution.py:342
  17.8 9.2 %collective-permute-start.7 = (f32[232,256]{1,0:T(8,128)S(1)}, f32[232,256]{1,0:T(8,128)S(1)}, u32[]{:S(2)}, u32[]{:S(2)}) collective-permute-start(f32[232,256]{1,0:T(8,128)S(1)} %get-tuple-element.42), channel_id=1, source_target_pairs={{0,2},{1,3},{2,0},{3,1},{4,6},{5,7},{6,4},{7,5},{8,10},{9,11},{10,... | collective-permute-start | bytes 712712 | tf_op jit(solution)/shard_map/ppermute | solution.py:342
  19.4 10.0 %collective-permute-start.6 = (f32[224,256]{1,0:T(8,128)S(1)}, f32[224,256]{1,0:T(8,128)S(1)}, u32[]{:S(2)}, u32[]{:S(2)}) collective-permute-start(f32[224,256]{1,0:T(8,128)S(1)} %get-tuple-element.39), channel_id=1, source_target_pairs={{0,1},{1,0},{2,3},{3,2},{4,5},{5,4},{6,7},{7,6},{8,9},{9,8},{10,11... | collective-permute-start | bytes 688136 | tf_op jit(solution)/shard_map/ppermute | solution.py:342
  24.8 7.1 %collective-permute-start.1 = (f32[136,256]{1,0:T(8,128)S(1)}, f32[136,256]{1,0:T(8,128)S(1)}, u32[]{:S(2)}, u32[]{:S(2)}) collective-permute-start(f32[136,256]{1,0:T(8,128)S(1)} %get-tuple-element.33), channel_id=1, source_target_pairs={{0,2},{1,3},{2,0},{3,1},{4,6},{5,7},{6,4},{7,5},{8,10},{9,11},{10,... | collective-permute-start | bytes 417800 | tf_op jit(solution)/shard_map/ppermute | solution.py:342
  27.4 7.5 %collective-permute-start.8 = (f32[136,256]{1,0:T(8,128)S(1)}, f32[136,256]{1,0:T(8,128)S(1)}, u32[]{:S(2)}, u32[]{:S(2)}) collective-permute-start(f32[136,256]{1,0:T(8,128)S(1)} %get-tuple-element.44), channel_id=1, source_target_pairs={{0,1},{1,0},{2,3},{3,2},{4,5},{5,4},{6,7},{7,6},{8,9},{9,8},{10,11... | collective-permute-start | bytes 417800 | tf_op jit(solution)/shard_map/ppermute | solution.py:342
  29.7 5.8 %collective-permute-start.10 = (f32[128,256]{1,0:T(8,128)S(1)}, f32[128,256]{1,0:T(8,128)S(1)}, u32[]{:S(2)}, u32[]{:S(2)}) collective-permute-start(f32[128,256]{1,0:T(8,128)S(1)} %get-tuple-element.49), channel_id=1, source_target_pairs={{0,2},{1,3},{2,0},{3,1},{4,6},{5,7},{6,4},{7,5},{8,10},{9,11},{10,... | collective-permute-start | bytes 393224 | tf_op jit(solution)/shard_map/ppermute | solution.py:342
  32.2 8.2 %collective-permute-start.2 = (f32[72,256]{1,0:T(8,128)S(1)}, f32[72,256]{1,0:T(8,128)S(1)}, u32[]{:S(2)}, u32[]{:S(2)}) collective-permute-start(f32[72,256]{1,0:T(8,128)S(1)} %get-tuple-element.35), channel_id=1, source_target_pairs={{0,4},{1,5},{2,6},{3,7},{4,0},{5,1},{6,2},{7,3},{8,12},{9,13},{10,... | collective-permute-start | bytes 221192 | tf_op jit(solution)/shard_map/ppermute | solution.py:342
  35.9 8.7 %collective-permute-start.11 = (f32[64,256]{1,0:T(8,128)S(1)}, f32[64,256]{1,0:T(8,128)S(1)}, u32[]{:S(2)}, u32[]{:S(2)}) collective-permute-start(f32[64,256]{1,0:T(8,128)S(1)} %get-tuple-element.51), channel_id=1, source_target_pairs={{0,4},{1,5},{2,6},{3,7},{4,0},{5,1},{6,2},{7,3},{8,12},{9,13},{10,... | collective-permute-start | bytes 196616 | tf_op jit(solution)/shard_map/ppermute | solution.py:342
  38.7 5.9 %collective-permute-start.9 = (f32[64,256]{1,0:T(8,128)S(1)}, f32[64,256]{1,0:T(8,128)S(1)}, u32[]{:S(2)}, u32[]{:S(2)}) collective-permute-start(f32[64,256]{1,0:T(8,128)S(1)} %get-tuple-element.47), channel_id=1, source_target_pairs={{0,4},{1,5},{2,6},{3,7},{4,0},{5,1},{6,2},{7,3},{8,12},{9,13},{10,... | collective-permute-start | bytes 196616 | tf_op jit(solution)/shard_map/ppermute | solution.py:342
  41.3 3.3 %collective-permute-start.5 = (f32[8,128]{1,0:T(8,128)S(1)}, f32[8,128]{1,0:T(8,128)S(1)}, u32[]{:S(2)}, u32[]{:S(2)}) collective-permute-start(f32[8,128]{1,0:T(8,128)S(1)} %shard_map.71.refs_0_), channel_id=1, source_target_pairs={{0,24},{8,16},{16,8},{24,0},{1,25},{9,17},{17,9},{25,1},{2,26},{10... | collective-permute-start | bytes 12296 | tf_op jit(solution)/shard_map/ppermute | solution.py:374
  41.4 3.7 %collective-permute-start.4 = (f32[8,128]{1,0:T(8,128)S(1)}, f32[8,128]{1,0:T(8,128)S(1)}, u32[]{:S(2)}, u32[]{:S(2)}) collective-permute-start(f32[8,128]{1,0:T(8,128)S(1)} %shard_map.71.refs_0_), channel_id=1, source_target_pairs={{0,16},{8,24},{16,0},{24,8},{1,17},{9,25},{17,1},{25,9},{2,18},{10... | collective-permute-start | bytes 12296 | tf_op jit(solution)/shard_map/ppermute | solution.py:374
  43.0 2.0 %collective-permute-start.3 = (f32[8,128]{1,0:T(8,128)S(1)}, f32[8,128]{1,0:T(8,128)S(1)}, u32[]{:S(2)}, u32[]{:S(2)}) collective-permute-start(f32[8,128]{1,0:T(8,128)S(1)} %shard_map.71.refs_0_), channel_id=1, source_target_pairs={{0,8},{8,0},{16,24},{24,16},{1,9},{9,1},{17,25},{25,17},{2,10},{10... | collective-permute-start | bytes 12296 | tf_op jit(solution)/shard_map/ppermute | solution.py:374
where the time goes:
time: 46.6 us; the launch traced here: 46.4 us
  Pallas kernels  19.1 us (41%)
  starting transfers between devices  18.6 us (40%)
  waiting for transfers between devices  7.37 us (16%)
  between operations  0.71 us (2%)
  local copies, waits for them, and re-layouts  0.66 us (1%)
    ppermute x9, starting transfers between devices, swap(): return lax.ppermute(array, 'bank', [(i, i ^ step) for i in range(banks)])  16.7 us
    pallas_call x1, Pallas kernels, on_device(): call(functools.partial(bank_kernel, plan, cols, firsts, carry), [SM, SM,...  13.5 us
    ppermute x9, waiting for transfers between devices, swap(): return lax.ppermute(array, 'bank', [(i, i ^ step) for i in range(banks)])  6.95 us
    pallas_call x6, Pallas kernels, merge(): call(functools.partial(merge_kernel, plan, picks, has_tile), [SM] + [VM]...  1.95 us
    ppermute x3, starting transfers between devices, on_device(): lax.ppermute(conf, 'img', [(i, i ^ s) for i in range(groups)])  1.92 us
    pallas_call x1, Pallas kernels, on_device(): call(functools.partial(final_kernel, plan, chunks, groups), [SM, SM, VM,...  1.4 us
    pallas_call x1, Pallas kernels, on_device(): call(functools.partial(prep_kernel, plan), [SM, SM, VM] + [VM] * far, [((...  1.4 us
  transfers between devices with their start and end apart: 12, of which 5 were waited for; matrix products, arithmetic and copies ran while one was open for 0% of the time, Pallas kernels for 9%

commit v1 on v0

--- a/solution.py
+++ b/solution.py
@@ -203,8 +203,7 @@
             out_ref[end:end + 8, :] = jnp.concatenate([peak, mass, peak, mass], axis=0)
 
 
-def conf_kernel(plan, cnt_ref, keep_ref, *refs):
-    out_ref = refs[-1]
+def live_kernel(plan, cnt_ref, keep_ref, live_ref):
     base, boxes = plan.base, plan.boxes
     li = long_image(cnt_ref)
     keep_l = (keep_ref[pl.ds(li, 1), :] == 1).astype(F32)
@@ -213,9 +212,15 @@
     turned = jnp.dot(jnp.broadcast_to(keep_s, (8, boxes)).astype(BF16), turn,
                      preferred_element_type=F32)[0:1, :]
     lane = iota((1, boxes), 1)
-    live = jnp.concatenate([jnp.where(lane < cnt_ref[0, li], keep_l, turned),
-                            jnp.where(lane < base, keep_s, 0.0)], axis=0)
+    live_ref[0:1, :] = jnp.where(lane < cnt_ref[0, li], keep_l, turned)
+    live_ref[1:2, :] = jnp.where(lane < base, keep_s, 0.0)
+    live_ref[2:8, :] = jnp.zeros((6, boxes), F32)
+
+
+def conf_kernel(live_ref, *refs):
+    out_ref = refs[-1]
     _, _, mass = merge_stats([r[...] for r in refs[:-1]])
+    live = live_ref[0:2, :]
     row = jnp.where(live > 0.5, -jnp.log(jnp.where(live > 0.5, mass, 1.0)), 0.0)
     total, count = jnp.sum(row), jnp.sum(live)
     out_ref[...] = jnp.where(iota((8, 128), 0) == 0, total, count)
@@ -349,6 +354,8 @@
             number * rows * cols * 4, number * rows * cols * 16, 8,
         )(pos, *arrays)
 
+    live, = call(functools.partial(live_kernel, plan), [SM, VM], [((8, slots), F32)], [],
+                 slots * 8, slots * 64, 4)(counts, keep)
     got = [swap(parts[2 * c + 1], 1 << firsts[c]) for c in range(chunks)]
     first_tile = {firsts[c]: got[c][plan.half_rows(firsts[c]):] for c in range(chunks) if carry[c]}
     quarters = plan.quarter_rows()
@@ -363,14 +370,16 @@
     pulls = []
     for c, bit in enumerate(firsts):
         own, seen = second[c]
+        if c == 0:
+            own, live = lax.optimization_barrier((own, live))
         if c == chunks - 1 and c > 0:
             own, pulls[-1][0] = lax.optimization_barrier((own, pulls[-1][0]))
         outs = merge(plan.own_picks, far, 2 * share, c == 0, own, seen, *second_tiles[bit])
         pulls.append([outs[0]] + [swap(outs[s], near * s) for s in range(1, far)])
     tiles = [p[2 * share:] for p in pulls[0]]
 
-    conf, = call(functools.partial(conf_kernel, plan), [SM, VM] + [VM] * far, [((8, 128), F32)], [],
-                 slots * 8, slots * 64, 4)(counts, keep, *tiles)
+    conf, = call(conf_kernel, [VM] * (1 + far), [((8, 128), F32)], [],
+                 slots * 8, slots * 64, 4)(live, *tiles)
     confs = [conf] + [lax.ppermute(conf, "img", [(i, i ^ s) for i in range(groups)])
                       for s in range(1, groups)]
     col, neg, log_norm = call(

time: 46.6 us -> 46.5 us (level)
  transfers between devices with their start and end apart: 12 -> 12, of which waited for: 5 -> 4; matrix products, arithmetic and copies ran while one was open for 0% -> 0% of each run, Pallas kernels for 9% -> 9%
where the time goes in v1:
time: 46.5 us; the launch traced here: 46.3 us
  Pallas kernels  19.1 us (41%)
  starting transfers between devices  18.6 us (40%)
  waiting for transfers between devices  7.2 us (15%)
  between operations  0.73 us (2%)
  local copies, waits for them, and re-layouts  0.67 us (1%)
    ppermute x9, starting transfers between devices, swap(): return lax.ppermute(array, 'bank', [(i, i ^ step) for i in range(banks)])  16.7 us
    pallas_call x1, Pallas kernels, on_device(): call(functools.partial(bank_kernel, plan, cols, firsts, carry), [SM, SM,...  13.5 us
    ppermute x9, waiting for transfers between devices, swap(): return lax.ppermute(array, 'bank', [(i, i ^ step) for i in range(banks)])  6.78 us
    pallas_call x6, Pallas kernels, merge(): call(functools.partial(merge_kernel, plan, picks, has_tile), [SM] + [VM]...  1.95 us
    ppermute x3, starting transfers between devices, on_device(): lax.ppermute(conf, 'img', [(i, i ^ s) for i in range(groups)])  1.92 us
    pallas_call x1, Pallas kernels, on_device(): call(functools.partial(final_kernel, plan, chunks, groups), [SM, SM, VM,...  1.4 us
    pallas_call x1, Pallas kernels, on_device(): call(functools.partial(prep_kernel, plan), [SM, SM, VM] + [VM] * far, [((...  1.4 us
  transfers between devices with their start and end apart: 12, of which 4 were waited for; matrix products, arithmetic and copies ran while one was open for 0% of the time, Pallas kernels for 9%

profile of v1, /device:TPU:0, one launch (start us, length us, event | category | flops | bytes accessed | tf_op | source)
XLA Modules:
  0.0 46.3 jit_solution(13174435403716135522)
XLA Ops:
  0.6 0.6 %copy-done.1 = s32[1,2]{1,0:T(1,128)S(1)} copy-done((s32[1,2]{1,0:T(1,128)S(1)}, s32[1,2]{1,0:T(1,128)}, u32[]{:S(2)}) %copy-start.1) | copy-done | bytes 32
  1.3 13.5 %shard_map.67 = (f32[8,256]{1,0:T(8,128)S(1)}, f32[224,256]{1,0:T(8,128)S(1)}, f32[232,256]{1,0:T(8,128)S(1)}, f32[224,256]{1,0:T(8,128)S(1)}, f32[232,256]{1,0:...) custom-call(s32[1,2]{1,0:T(1,128)S(1)} %copy-done.1, s32[1]{0:T(128)} %bitcast.pos_ref, ...), custom_call_target="tpu_custom_call" | custom-call | flops 8053063680 | bytes 12582912 | tf_op jit(solution)/shard_map/pallas_call | solution.py:335
  14.8 3.0 %collective-permute-start = (f32[232,256]{1,0:T(8,128)S(1)}, f32[232,256]{1,0:T(8,128)S(1)}, u32[]{:S(2)}, u32[]{:S(2)}) collective-permute-start(f32[232,256]{1,0:T(8,128)S(1)} %get-tuple-element.32), channel_id=1, source_target_pairs={{0,1},{1,0},{2,3},{3,2},{4,5},{5,4},{6,7},{7,6},{8,9},{9,8},{10,11... | collective-permute-start | bytes 712712 | tf_op jit(solution)/shard_map/ppermute | solution.py:347
  17.8 1.6 %collective-permute-start.7 = (f32[232,256]{1,0:T(8,128)S(1)}, f32[232,256]{1,0:T(8,128)S(1)}, u32[]{:S(2)}, u32[]{:S(2)}) collective-permute-start(f32[232,256]{1,0:T(8,128)S(1)} %get-tuple-element.46), channel_id=1, source_target_pairs={{0,2},{1,3},{2,0},{3,1},{4,6},{5,7},{6,4},{7,5},{8,10},{9,11},{10,... | collective-permute-start | bytes 712712 | tf_op jit(solution)/shard_map/ppermute | solution.py:347
  19.4 0.5 %collective-permute-start.6 = (f32[224,256]{1,0:T(8,128)S(1)}, f32[224,256]{1,0:T(8,128)S(1)}, u32[]{:S(2)}, u32[]{:S(2)}) collective-permute-start(f32[224,256]{1,0:T(8,128)S(1)} %get-tuple-element.43), channel_id=1, source_target_pairs={{0,1},{1,0},{2,3},{3,2},{4,5},{5,4},{6,7},{7,6},{8,9},{9,8},{10,11... | collective-permute-start | bytes 688136 | tf_op jit(solution)/shard_map/ppermute | solution.py:347
  20.0 4.5 %collective-permute-done.got_ref = f32[232,256]{1,0:T(8,128)S(1)} collective-permute-done((f32[232,256]{1,0:T(8,128)S(1)}, f32[232,256]{1,0:T(8,128)S(1)}, u32[]{:S(2)}, u32[]{:S(2)}) %collective-permute-start) | collective-permute-done | bytes 237600 | tf_op jit(solution)/shard_map/ppermute | solution.py:347
  24.5 0.4 shard_map.68
  24.8 2.2 %collective-permute-start.1 = (f32[136,256]{1,0:T(8,128)S(1)}, f32[136,256]{1,0:T(8,128)S(1)}, u32[]{:S(2)}, u32[]{:S(2)}) collective-permute-start(f32[136,256]{1,0:T(8,128)S(1)} %get-tuple-element.36), channel_id=1, source_target_pairs={{0,2},{1,3},{2,0},{3,1},{4,6},{5,7},{6,4},{7,5},{8,10},{9,11},{10,... | collective-permute-start | bytes 417800 | tf_op jit(solution)/shard_map/ppermute | solution.py:347
  27.0 0.0 collective-permute-done.7.got_ref
  27.0 0.4 shard_map.74
  27.4 1.6 %collective-permute-start.8 = (f32[136,256]{1,0:T(8,128)S(1)}, f32[136,256]{1,0:T(8,128)S(1)}, u32[]{:S(2)}, u32[]{:S(2)}) collective-permute-start(f32[136,256]{1,0:T(8,128)S(1)} %get-tuple-element.48), channel_id=1, source_target_pairs={{0,1},{1,0},{2,3},{3,2},{4,5},{5,4},{6,7},{7,6},{8,9},{9,8},{10,11... | collective-permute-start | bytes 417800 | tf_op jit(solution)/shard_map/ppermute | solution.py:347
  28.9 0.5 %collective-permute-done.6.got_ref = f32[224,256]{1,0:T(8,128)S(1)} collective-permute-done((f32[224,256]{1,0:T(8,128)S(1)}, f32[224,256]{1,0:T(8,128)S(1)}, u32[]{:S(2)}, u32[]{:S(2)}) %collective-permute-start.6) | collective-permute-done | bytes 229408 | tf_op jit(solution)/shard_map/ppermute | solution.py:347
  29.4 0.3 shard_map.73
  29.7 2.2 %collective-permute-start.10 = (f32[128,256]{1,0:T(8,128)S(1)}, f32[128,256]{1,0:T(8,128)S(1)}, u32[]{:S(2)}, u32[]{:S(2)}) collective-permute-start(f32[128,256]{1,0:T(8,128)S(1)} %get-tuple-element.53), channel_id=1, source_target_pairs={{0,2},{1,3},{2,0},{3,1},{4,6},{5,7},{6,4},{7,5},{8,10},{9,11},{10,... | collective-permute-start | bytes 393224 | tf_op jit(solution)/shard_map/ppermute | solution.py:347
  31.9 0.7 %shard_map.69.live_ref = f32[8,256]{1,0:T(8,128)S(1)} custom-call(s32[1,2]{1,0:T(1,128)S(1)} %copy-done.1, s32[2,256]{1,0:T(2,128)S(1)} %copy-done), custom_call_target="tpu_custom_call" | custom-call | flops 2048 | bytes 16384 | tf_op jit(solution)/shard_map/pallas_call | solution.py:357
  32.6 0.0 collective-permute-done.1.got_ref
  32.6 0.3 shard_map.70
  32.9 2.7 %collective-permute-start.2 = (f32[72,256]{1,0:T(8,128)S(1)}, f32[72,256]{1,0:T(8,128)S(1)}, u32[]{:S(2)}, u32[]{:S(2)}) collective-permute-start(f32[72,256]{1,0:T(8,128)S(1)} %get-tuple-element.38), channel_id=1, source_target_pairs={{0,4},{1,5},{2,6},{3,7},{4,0},{5,1},{6,2},{7,3},{8,12},{9,13},{10,... | collective-permute-start | bytes 221192 | tf_op jit(solution)/shard_map/ppermute | solution.py:347
  35.6 0.0 collective-permute-done.8.got_ref
  35.6 0.3 shard_map.75
  35.9 0.0 collective-permute-done.10.got_ref
  35.9 0.3 shard_map.76
  36.2 2.4 %collective-permute-start.11 = (f32[64,256]{1,0:T(8,128)S(1)}, f32[64,256]{1,0:T(8,128)S(1)}, u32[]{:S(2)}, u32[]{:S(2)}) collective-permute-start(f32[64,256]{1,0:T(8,128)S(1)} %get-tuple-element.55), channel_id=1, source_target_pairs={{0,4},{1,5},{2,6},{3,7},{4,0},{5,1},{6,2},{7,3},{8,12},{9,13},{10,... | collective-permute-start | bytes 196616 | tf_op jit(solution)/shard_map/ppermute | solution.py:347
  38.6 0.6 %collective-permute-start.9 = (f32[64,256]{1,0:T(8,128)S(1)}, f32[64,256]{1,0:T(8,128)S(1)}, u32[]{:S(2)}, u32[]{:S(2)}) collective-permute-start(f32[64,256]{1,0:T(8,128)S(1)} %get-tuple-element.51), channel_id=1, source_target_pairs={{0,4},{1,5},{2,6},{3,7},{4,0},{5,1},{6,2},{7,3},{8,12},{9,13},{10,... | collective-permute-start | bytes 196616 | tf_op jit(solution)/shard_map/ppermute | solution.py:347
  39.2 1.8 %collective-permute-done.2.refs_5_ = f32[72,256]{1,0:T(8,128)S(1)} collective-permute-done((f32[72,256]{1,0:T(8,128)S(1)}, f32[72,256]{1,0:T(8,128)S(1)}, u32[]{:S(2)}, u32[]{:S(2)}) %collective-permute-start.2) | collective-permute-done | bytes 73760 | tf_op jit(solution)/shard_map/ppermute | solution.py:347
  41.0 0.1 shard_map.72.refs_0_
  41.1 0.1 collective-permute-start.5
  41.2 1.6 %collective-permute-start.4 = (f32[8,128]{1,0:T(8,128)S(1)}, f32[8,128]{1,0:T(8,128)S(1)}, u32[]{:S(2)}, u32[]{:S(2)}) collective-permute-start(f32[8,128]{1,0:T(8,128)S(1)} %shard_map.72.refs_0_), channel_id=1, source_target_pairs={{0,16},{8,24},{16,0},{24,8},{1,17},{9,25},{17,1},{25,9},{2,18},{10... | collective-permute-start | bytes 12296 | tf_op jit(solution)/shard_map/ppermute | solution.py:383
  42.8 0.3 collective-permute-start.3
  43.1 1.4 %shard_map.71 = (f32[64,128]{1,0:T(8,128)S(1)}, f32[8,128]{1,0:T(8,128)S(1)}, f32[2,32]{1,0:T(2,128)}) custom-call(s32[1,2]{1,0:T(1,128)S(1)} %copy-done.1, s32[1]{0:T(128)} %bitcast.pos_ref, s32[2,256]{1,0:T(2,128)S(1)} %copy-done, f32[8,256]{1,0:T(8,128)S(1)} %slice.27.refs_0_, f32[8,256]{1,0:T(8,128)S(1)} %slice.34.refs_1_), custom_call_target="tpu_custom_call" | custom-call | flops 2048 | bytes 16384 | tf_op jit(solution)/shard_map/pallas_call | solution.py:385
  44.5 0.4 collective-permute-done.4.refs_2_
  44.9 1.4 %shard_map.77 = (bf16[2,32,768]{2,1,0:T(8,128)(2,1)}, f32[2,32]{1,0:T(2,128)}) custom-call(s32[1,2]{1,0:T(1,128)S(1)} %copy-done.1, s32[1]{0:T(128)} %bitcast.pos_ref, f32[64,128]{1,0:T(8,128)S(1)} %get-tuple-element.39.col_ref, f32[8,128]{1,0:T(8,128)S(1)} %get-tuple-element.40.neg_ref, f32[8,128]{1,0:T(8,128)S(1)} %shard_map.72.refs_0_, ...), custom_call_target="tpu_custom_call" | custom-call | flops 196608 | bytes 393216 | tf_op jit(solution)/shard_map/pallas_call | solution.py:391
  (15 shorter events, 0.0 us)
Async XLA Ops:
  0.6 0.7 %copy-start.1 = (s32[1,2]{1,0:T(1,128)S(1)}, s32[1,2]{1,0:T(1,128)}, u32[]{:S(2)}) copy-start(s32[1,2]{1,0:T(1,128)} %cnt_ref.7) | copy-start | bytes 28
  1.3 30.6 %copy-start = (s32[2,256]{1,0:T(2,128)S(1)}, s32[2,256]{1,0:T(2,128)}, u32[]{:S(2)}) copy-start(s32[2,256]{1,0:T(2,128)} %keep_ref.3) | copy-start | bytes 6148
  14.8 9.7 %collective-permute-start = (f32[232,256]{1,0:T(8,128)S(1)}, f32[232,256]{1,0:T(8,128)S(1)}, u32[]{:S(2)}, u32[]{:S(2)}) collective-permute-start(f32[232,256]{1,0:T(8,128)S(1)} %get-tuple-element.32), channel_id=1, source_target_pairs={{0,1},{1,0},{2,3},{3,2},{4,5},{5,4},{6,7},{7,6},{8,9},{9,8},{10,11... | collective-permute-start | bytes 712712 | tf_op jit(solution)/shard_map/ppermute | solution.py:347
  17.8 9.2 %collective-permute-start.7 = (f32[232,256]{1,0:T(8,128)S(1)}, f32[232,256]{1,0:T(8,128)S(1)}, u32[]{:S(2)}, u32[]{:S(2)}) collective-permute-start(f32[232,256]{1,0:T(8,128)S(1)} %get-tuple-element.46), channel_id=1, source_target_pairs={{0,2},{1,3},{2,0},{3,1},{4,6},{5,7},{6,4},{7,5},{8,10},{9,11},{10,... | collective-permute-start | bytes 712712 | tf_op jit(solution)/shard_map/ppermute | solution.py:347
  19.4 10.0 %collective-permute-start.6 = (f32[224,256]{1,0:T(8,128)S(1)}, f32[224,256]{1,0:T(8,128)S(1)}, u32[]{:S(2)}, u32[]{:S(2)}) collective-permute-start(f32[224,256]{1,0:T(8,128)S(1)} %get-tuple-element.43), channel_id=1, source_target_pairs={{0,1},{1,0},{2,3},{3,2},{4,5},{5,4},{6,7},{7,6},{8,9},{9,8},{10,11... | collective-permute-start | bytes 688136 | tf_op jit(solution)/shard_map/ppermute | solution.py:347
  24.8 7.8 %collective-permute-start.1 = (f32[136,256]{1,0:T(8,128)S(1)}, f32[136,256]{1,0:T(8,128)S(1)}, u32[]{:S(2)}, u32[]{:S(2)}) collective-permute-start(f32[136,256]{1,0:T(8,128)S(1)} %get-tuple-element.36), channel_id=1, source_target_pairs={{0,2},{1,3},{2,0},{3,1},{4,6},{5,7},{6,4},{7,5},{8,10},{9,11},{10,... | collective-permute-start | bytes 417800 | tf_op jit(solution)/shard_map/ppermute | solution.py:347
  27.4 8.2 %collective-permute-start.8 = (f32[136,256]{1,0:T(8,128)S(1)}, f32[136,256]{1,0:T(8,128)S(1)}, u32[]{:S(2)}, u32[]{:S(2)}) collective-permute-start(f32[136,256]{1,0:T(8,128)S(1)} %get-tuple-element.48), channel_id=1, source_target_pairs={{0,1},{1,0},{2,3},{3,2},{4,5},{5,4},{6,7},{7,6},{8,9},{9,8},{10,11... | collective-permute-start | bytes 417800 | tf_op jit(solution)/shard_map/ppermute | solution.py:347
  29.7 6.2 %collective-permute-start.10 = (f32[128,256]{1,0:T(8,128)S(1)}, f32[128,256]{1,0:T(8,128)S(1)}, u32[]{:S(2)}, u32[]{:S(2)}) collective-permute-start(f32[128,256]{1,0:T(8,128)S(1)} %get-tuple-element.53), channel_id=1, source_target_pairs={{0,2},{1,3},{2,0},{3,1},{4,6},{5,7},{6,4},{7,5},{8,10},{9,11},{10,... | collective-permute-start | bytes 393224 | tf_op jit(solution)/shard_map/ppermute | solution.py:347
  32.9 8.1 %collective-permute-start.2 = (f32[72,256]{1,0:T(8,128)S(1)}, f32[72,256]{1,0:T(8,128)S(1)}, u32[]{:S(2)}, u32[]{:S(2)}) collective-permute-start(f32[72,256]{1,0:T(8,128)S(1)} %get-tuple-element.38), channel_id=1, source_target_pairs={{0,4},{1,5},{2,6},{3,7},{4,0},{5,1},{6,2},{7,3},{8,12},{9,13},{10,... | collective-permute-start | bytes 221192 | tf_op jit(solution)/shard_map/ppermute | solution.py:347
  36.2 8.3 %collective-permute-start.11 = (f32[64,256]{1,0:T(8,128)S(1)}, f32[64,256]{1,0:T(8,128)S(1)}, u32[]{:S(2)}, u32[]{:S(2)}) collective-permute-start(f32[64,256]{1,0:T(8,128)S(1)} %get-tuple-element.55), channel_id=1, source_target_pairs={{0,4},{1,5},{2,6},{3,7},{4,0},{5,1},{6,2},{7,3},{8,12},{9,13},{10,... | collective-permute-start | bytes 196616 | tf_op jit(solution)/shard_map/ppermute | solution.py:347
  38.6 5.8 %collective-permute-start.9 = (f32[64,256]{1,0:T(8,128)S(1)}, f32[64,256]{1,0:T(8,128)S(1)}, u32[]{:S(2)}, u32[]{:S(2)}) collective-permute-start(f32[64,256]{1,0:T(8,128)S(1)} %get-tuple-element.51), channel_id=1, source_target_pairs={{0,4},{1,5},{2,6},{3,7},{4,0},{5,1},{6,2},{7,3},{8,12},{9,13},{10,... | collective-permute-start | bytes 196616 | tf_op jit(solution)/shard_map/ppermute | solution.py:347
  41.1 3.3 %collective-permute-start.5 = (f32[8,128]{1,0:T(8,128)S(1)}, f32[8,128]{1,0:T(8,128)S(1)}, u32[]{:S(2)}, u32[]{:S(2)}) collective-permute-start(f32[8,128]{1,0:T(8,128)S(1)} %shard_map.72.refs_0_), channel_id=1, source_target_pairs={{0,24},{8,16},{16,8},{24,0},{1,25},{9,17},{17,9},{25,1},{2,26},{10... | collective-permute-start | bytes 12296 | tf_op jit(solution)/shard_map/ppermute | solution.py:383
  41.2 3.7 %collective-permute-start.4 = (f32[8,128]{1,0:T(8,128)S(1)}, f32[8,128]{1,0:T(8,128)S(1)}, u32[]{:S(2)}, u32[]{:S(2)}) collective-permute-start(f32[8,128]{1,0:T(8,128)S(1)} %shard_map.72.refs_0_), channel_id=1, source_target_pairs={{0,16},{8,24},{16,0},{24,8},{1,17},{9,25},{17,1},{25,9},{2,18},{10... | collective-permute-start | bytes 12296 | tf_op jit(solution)/shard_map/ppermute | solution.py:383
  42.8 2.1 %collective-permute-start.3 = (f32[8,128]{1,0:T(8,128)S(1)}, f32[8,128]{1,0:T(8,128)S(1)}, u32[]{:S(2)}, u32[]{:S(2)}) collective-permute-start(f32[8,128]{1,0:T(8,128)S(1)} %shard_map.72.refs_0_), channel_id=1, source_target_pairs={{0,8},{8,0},{16,24},{24,16},{1,9},{9,1},{17,25},{25,17},{2,10},{10... | collective-permute-start | bytes 12296 | tf_op jit(solution)/shard_map/ppermute | solution.py:383

commit v2 on v1

--- a/solution.py
+++ b/solution.py
@@ -301,7 +301,7 @@
 HBM = pl.BlockSpec(memory_space=pltpu.HBM)
 MIB = 2**20
 VMEM_MIB = 52
-FIRST_BIT = (0, 1, 0)
+FIRST_BIT = (0, 0, 1)
 
 
 def call(body, ins, outs, scratch, flops, moved, limit, out_specs=None):
@@ -357,6 +357,7 @@
     live, = call(functools.partial(live_kernel, plan), [SM, VM], [((8, slots), F32)], [],
                  slots * 8, slots * 64, 4)(counts, keep)
     got = [swap(parts[2 * c + 1], 1 << firsts[c]) for c in range(chunks)]
+    got[0], live = lax.optimization_barrier((got[0], live))
     first_tile = {firsts[c]: got[c][plan.half_rows(firsts[c]):] for c in range(chunks) if carry[c]}
     quarters = plan.quarter_rows()
     second_tiles = {}
@@ -370,8 +371,6 @@
     pulls = []
     for c, bit in enumerate(firsts):
         own, seen = second[c]
-        if c == 0:
-            own, live = lax.optimization_barrier((own, live))
         if c == chunks - 1 and c > 0:
             own, pulls[-1][0] = lax.optimization_barrier((own, pulls[-1][0]))
         outs = merge(plan.own_picks, far, 2 * share, c == 0, own, seen, *second_tiles[bit])

time: 46.5 us -> 46.5 us (level)
  transfers between devices with their start and end apart: 12 -> 12, of which waited for: 4 -> 5; matrix products, arithmetic and copies ran while one was open for 0% -> 0% of each run, Pallas kernels for 9% -> 9%
where the time goes in v2:
time: 46.5 us; the launch traced here: 46.3 us
  Pallas kernels  19.1 us (41%)
  starting transfers between devices  18.7 us (40%)
  waiting for transfers between devices  7.23 us (16%)
  between operations  0.72 us (2%)
  local copies, waits for them, and re-layouts  0.66 us (1%)
    ppermute x9, starting transfers between devices, swap(): return lax.ppermute(array, 'bank', [(i, i ^ step) for i in range(banks)])  16.8 us
    pallas_call x1, Pallas kernels, on_device(): call(functools.partial(bank_kernel, plan, cols, firsts, carry), [SM, SM,...  13.5 us
    ppermute x9, waiting for transfers between devices, swap(): return lax.ppermute(array, 'bank', [(i, i ^ step) for i in range(banks)])  7.22 us
    pallas_call x6, Pallas kernels, merge(): call(functools.partial(merge_kernel, plan, picks, has_tile), [SM] + [VM]...  1.95 us
    ppermute x3, starting transfers between devices, on_device(): lax.ppermute(conf, 'img', [(i, i ^ s) for i in range(groups)])  1.92 us
    pallas_call x1, Pallas kernels, on_device(): call(functools.partial(final_kernel, plan, chunks, groups), [SM, SM, VM,...  1.4 us
    pallas_call x1, Pallas kernels, on_device(): call(functools.partial(prep_kernel, plan), [SM, SM, VM] + [VM] * far, [((...  1.4 us
  transfers between devices with their start and end apart: 12, of which 5 were waited for; matrix products, arithmetic and copies ran while one was open for 0% of the time, Pallas kernels for 9%

profile of v2, /device:TPU:0, one launch (start us, length us, event | category | flops | bytes accessed | tf_op | source)
XLA Modules:
  0.0 46.3 jit_solution(16209507227185609797)
XLA Ops:
  0.6 0.6 %copy-done.1 = s32[1,2]{1,0:T(1,128)S(1)} copy-done((s32[1,2]{1,0:T(1,128)S(1)}, s32[1,2]{1,0:T(1,128)}, u32[]{:S(2)}) %copy-start.1) | copy-done | bytes 32
  1.3 13.5 %shard_map.67 = (f32[8,256]{1,0:T(8,128)S(1)}, f32[224,256]{1,0:T(8,128)S(1)}, f32[232,256]{1,0:T(8,128)S(1)}, f32[224,256]{1,0:T(8,128)S(1)}, f32[224,256]{1,0:...) custom-call(s32[1,2]{1,0:T(1,128)S(1)} %copy-done.1, s32[1]{0:T(128)} %bitcast.pos_ref, ...), custom_call_target="tpu_custom_call" | custom-call | flops 8053063680 | bytes 12582912 | tf_op jit(solution)/shard_map/pallas_call | solution.py:335
  14.8 3.0 %collective-permute-start = (f32[232,256]{1,0:T(8,128)S(1)}, f32[232,256]{1,0:T(8,128)S(1)}, u32[]{:S(2)}, u32[]{:S(2)}) collective-permute-start(f32[232,256]{1,0:T(8,128)S(1)} %get-tuple-element.32), channel_id=1, source_target_pairs={{0,1},{1,0},{2,3},{3,2},{4,5},{5,4},{6,7},{7,6},{8,9},{9,8},{10,11... | collective-permute-start | bytes 712712 | tf_op jit(solution)/shard_map/ppermute | solution.py:347
  17.8 1.6 %collective-permute-start.6 = (f32[232,256]{1,0:T(8,128)S(1)}, f32[232,256]{1,0:T(8,128)S(1)}, u32[]{:S(2)}, u32[]{:S(2)}) collective-permute-start(f32[232,256]{1,0:T(8,128)S(1)} %get-tuple-element.43), channel_id=1, source_target_pairs={{0,2},{1,3},{2,0},{3,1},{4,6},{5,7},{6,4},{7,5},{8,10},{9,11},{10,... | collective-permute-start | bytes 712712 | tf_op jit(solution)/shard_map/ppermute | solution.py:347
  19.4 0.5 %collective-permute-start.7 = (f32[224,256]{1,0:T(8,128)S(1)}, f32[224,256]{1,0:T(8,128)S(1)}, u32[]{:S(2)}, u32[]{:S(2)}) collective-permute-start(f32[224,256]{1,0:T(8,128)S(1)} %get-tuple-element.46), channel_id=1, source_target_pairs={{0,1},{1,0},{2,3},{3,2},{4,5},{5,4},{6,7},{7,6},{8,9},{9,8},{10,11... | collective-permute-start | bytes 688136 | tf_op jit(solution)/shard_map/ppermute | solution.py:347
  19.9 0.7 %shard_map.68.live_ref = f32[8,256]{1,0:T(8,128)S(1)} custom-call(s32[1,2]{1,0:T(1,128)S(1)} %copy-done.1, s32[2,256]{1,0:T(2,128)S(1)} %copy-done), custom_call_target="tpu_custom_call" | custom-call | flops 2048 | bytes 16384 | tf_op jit(solution)/shard_map/pallas_call | solution.py:357
  20.6 3.8 %collective-permute-done.got_ref = f32[232,256]{1,0:T(8,128)S(1)} collective-permute-done((f32[232,256]{1,0:T(8,128)S(1)}, f32[232,256]{1,0:T(8,128)S(1)}, u32[]{:S(2)}, u32[]{:S(2)}) %collective-permute-start) | collective-permute-done | bytes 237600 | tf_op jit(solution)/shard_map/ppermute | solution.py:347
  24.5 0.4 shard_map.69
  24.8 2.2 %collective-permute-start.1 = (f32[136,256]{1,0:T(8,128)S(1)}, f32[136,256]{1,0:T(8,128)S(1)}, u32[]{:S(2)}, u32[]{:S(2)}) collective-permute-start(f32[136,256]{1,0:T(8,128)S(1)} %get-tuple-element.36), channel_id=1, source_target_pairs={{0,2},{1,3},{2,0},{3,1},{4,6},{5,7},{6,4},{7,5},{8,10},{9,11},{10,... | collective-permute-start | bytes 417800 | tf_op jit(solution)/shard_map/ppermute | solution.py:347
  27.0 0.4 shard_map.73
  27.3 1.6 %collective-permute-start.10 = (f32[136,256]{1,0:T(8,128)S(1)}, f32[136,256]{1,0:T(8,128)S(1)}, u32[]{:S(2)}, u32[]{:S(2)}) collective-permute-start(f32[136,256]{1,0:T(8,128)S(1)} %get-tuple-element.53), channel_id=1, source_target_pairs={{0,1},{1,0},{2,3},{3,2},{4,5},{5,4},{6,7},{7,6},{8,9},{9,8},{10,11... | collective-permute-start | bytes 417800 | tf_op jit(solution)/shard_map/ppermute | solution.py:347
  28.9 0.5 %collective-permute-done.7.got_ref = f32[224,256]{1,0:T(8,128)S(1)} collective-permute-done((f32[224,256]{1,0:T(8,128)S(1)}, f32[224,256]{1,0:T(8,128)S(1)}, u32[]{:S(2)}, u32[]{:S(2)}) %collective-permute-start.7) | collective-permute-done | bytes 229408 | tf_op jit(solution)/shard_map/ppermute | solution.py:347
  29.4 0.3 shard_map.74
  29.7 2.2 %collective-permute-start.8 = (f32[128,256]{1,0:T(8,128)S(1)}, f32[128,256]{1,0:T(8,128)S(1)}, u32[]{:S(2)}, u32[]{:S(2)}) collective-permute-start(f32[128,256]{1,0:T(8,128)S(1)} %get-tuple-element.48), channel_id=1, source_target_pairs={{0,2},{1,3},{2,0},{3,1},{4,6},{5,7},{6,4},{7,5},{8,10},{9,11},{10,... | collective-permute-start | bytes 393224 | tf_op jit(solution)/shard_map/ppermute | solution.py:347
  31.9 0.3 shard_map.70
  32.2 2.7 %collective-permute-start.2 = (f32[72,256]{1,0:T(8,128)S(1)}, f32[72,256]{1,0:T(8,128)S(1)}, u32[]{:S(2)}, u32[]{:S(2)}) collective-permute-start(f32[72,256]{1,0:T(8,128)S(1)} %get-tuple-element.38), channel_id=1, source_target_pairs={{0,4},{1,5},{2,6},{3,7},{4,0},{5,1},{6,2},{7,3},{8,12},{9,13},{10,... | collective-permute-start | bytes 221192 | tf_op jit(solution)/shard_map/ppermute | solution.py:347
  34.9 0.7 %collective-permute-done.8.got_ref = f32[128,256]{1,0:T(8,128)S(1)} collective-permute-done((f32[128,256]{1,0:T(8,128)S(1)}, f32[128,256]{1,0:T(8,128)S(1)}, u32[]{:S(2)}, u32[]{:S(2)}) %collective-permute-start.8) | collective-permute-done | bytes 131104 | tf_op jit(solution)/shard_map/ppermute | solution.py:347
  35.5 0.3 shard_map.75
  35.8 2.9 %collective-permute-start.9 = (f32[64,256]{1,0:T(8,128)S(1)}, f32[64,256]{1,0:T(8,128)S(1)}, u32[]{:S(2)}, u32[]{:S(2)}) collective-permute-start(f32[64,256]{1,0:T(8,128)S(1)} %get-tuple-element.51), channel_id=1, source_target_pairs={{0,4},{1,5},{2,6},{3,7},{4,0},{5,1},{6,2},{7,3},{8,12},{9,13},{10,... | collective-permute-start | bytes 196616 | tf_op jit(solution)/shard_map/ppermute | solution.py:347
  38.7 0.0 collective-permute-done.10.got_ref
  38.7 0.3 shard_map.76
  39.0 0.2 collective-permute-start.11
  39.2 0.2 collective-permute-done.2.refs_5_
  39.4 0.1 shard_map.72.refs_0_
  39.6 0.1 collective-permute-start.5
  39.6 1.5 %collective-permute-start.4 = (f32[8,128]{1,0:T(8,128)S(1)}, f32[8,128]{1,0:T(8,128)S(1)}, u32[]{:S(2)}, u32[]{:S(2)}) collective-permute-start(f32[8,128]{1,0:T(8,128)S(1)} %shard_map.72.refs_0_), channel_id=1, source_target_pairs={{0,16},{8,24},{16,0},{24,8},{1,17},{9,25},{17,1},{25,9},{2,18},{10... | collective-permute-start | bytes 12296 | tf_op jit(solution)/shard_map/ppermute | solution.py:382
  41.2 0.3 collective-permute-start.3
  41.5 1.4 %shard_map.71 = (f32[64,128]{1,0:T(8,128)S(1)}, f32[8,128]{1,0:T(8,128)S(1)}, f32[2,32]{1,0:T(2,128)}) custom-call(s32[1,2]{1,0:T(1,128)S(1)} %copy-done.1, s32[1]{0:T(128)} %bitcast.pos_ref, s32[2,256]{1,0:T(2,128)S(1)} %copy-done, f32[8,256]{1,0:T(8,128)S(1)} %slice.27.refs_0_, f32[8,256]{1,0:T(8,128)S(1)} %slice.33.refs_1_), custom_call_target="tpu_custom_call" | custom-call | flops 2048 | bytes 16384 | tf_op jit(solution)/shard_map/pallas_call | solution.py:384
  42.9 2.1 %collective-permute-done.11.refs_9_ = f32[64,256]{1,0:T(8,128)S(1)} collective-permute-done((f32[64,256]{1,0:T(8,128)S(1)}, f32[64,256]{1,0:T(8,128)S(1)}, u32[]{:S(2)}, u32[]{:S(2)}) %collective-permute-start.11) | collective-permute-done | bytes 65568 | tf_op jit(solution)/shard_map/ppermute | solution.py:347
  44.9 0.0 collective-permute-done.5.refs_3_
  44.9 0.0 collective-permute-done.4.refs_2_
  44.9 1.4 %shard_map.77 = (bf16[2,32,768]{2,1,0:T(8,128)(2,1)}, f32[2,32]{1,0:T(2,128)}) custom-call(s32[1,2]{1,0:T(1,128)S(1)} %copy-done.1, s32[1]{0:T(128)} %bitcast.pos_ref, f32[64,128]{1,0:T(8,128)S(1)} %get-tuple-element.39.col_ref, f32[8,128]{1,0:T(8,128)S(1)} %get-tuple-element.40.neg_ref, f32[8,128]{1,0:T(8,128)S(1)} %shard_map.72.refs_0_, ...), custom_call_target="tpu_custom_call" | custom-call | flops 196608 | bytes 393216 | tf_op jit(solution)/shard_map/pallas_call | solution.py:390
  (15 shorter events, 0.0 us)
Async XLA Ops:
  0.6 0.7 %copy-start.1 = (s32[1,2]{1,0:T(1,128)S(1)}, s32[1,2]{1,0:T(1,128)}, u32[]{:S(2)}) copy-start(s32[1,2]{1,0:T(1,128)} %cnt_ref.7) | copy-start | bytes 28
  1.3 18.6 %copy-start = (s32[2,256]{1,0:T(2,128)S(1)}, s32[2,256]{1,0:T(2,128)}, u32[]{:S(2)}) copy-start(s32[2,256]{1,0:T(2,128)} %keep_ref.3) | copy-start | bytes 6148
  14.8 9.7 %collective-permute-start = (f32[232,256]{1,0:T(8,128)S(1)}, f32[232,256]{1,0:T(8,128)S(1)}, u32[]{:S(2)}, u32[]{:S(2)}) collective-permute-start(f32[232,256]{1,0:T(8,128)S(1)} %get-tuple-element.32), channel_id=1, source_target_pairs={{0,1},{1,0},{2,3},{3,2},{4,5},{5,4},{6,7},{7,6},{8,9},{9,8},{10,11... | collective-permute-start | bytes 712712 | tf_op jit(solution)/shard_map/ppermute | solution.py:347
  17.8 9.2 %collective-permute-start.6 = (f32[232,256]{1,0:T(8,128)S(1)}, f32[232,256]{1,0:T(8,128)S(1)}, u32[]{:S(2)}, u32[]{:S(2)}) collective-permute-start(f32[232,256]{1,0:T(8,128)S(1)} %get-tuple-element.43), channel_id=1, source_target_pairs={{0,2},{1,3},{2,0},{3,1},{4,6},{5,7},{6,4},{7,5},{8,10},{9,11},{10,... | collective-permute-start | bytes 712712 | tf_op jit(solution)/shard_map/ppermute | solution.py:347
  19.4 10.0 %collective-permute-start.7 = (f32[224,256]{1,0:T(8,128)S(1)}, f32[224,256]{1,0:T(8,128)S(1)}, u32[]{:S(2)}, u32[]{:S(2)}) collective-permute-start(f32[224,256]{1,0:T(8,128)S(1)} %get-tuple-element.46), channel_id=1, source_target_pairs={{0,1},{1,0},{2,3},{3,2},{4,5},{5,4},{6,7},{7,6},{8,9},{9,8},{10,11... | collective-permute-start | bytes 688136 | tf_op jit(solution)/shard_map/ppermute | solution.py:347
  24.8 7.1 %collective-permute-start.1 = (f32[136,256]{1,0:T(8,128)S(1)}, f32[136,256]{1,0:T(8,128)S(1)}, u32[]{:S(2)}, u32[]{:S(2)}) collective-permute-start(f32[136,256]{1,0:T(8,128)S(1)} %get-tuple-element.36), channel_id=1, source_target_pairs={{0,2},{1,3},{2,0},{3,1},{4,6},{5,7},{6,4},{7,5},{8,10},{9,11},{10,... | collective-permute-start | bytes 417800 | tf_op jit(solution)/shard_map/ppermute | solution.py:347
  27.3 11.3 %collective-permute-start.10 = (f32[136,256]{1,0:T(8,128)S(1)}, f32[136,256]{1,0:T(8,128)S(1)}, u32[]{:S(2)}, u32[]{:S(2)}) collective-permute-start(f32[136,256]{1,0:T(8,128)S(1)} %get-tuple-element.53), channel_id=1, source_target_pairs={{0,1},{1,0},{2,3},{3,2},{4,5},{5,4},{6,7},{7,6},{8,9},{9,8},{10,11... | collective-permute-start | bytes 417800 | tf_op jit(solution)/shard_map/ppermute | solution.py:347
  29.7 5.8 %collective-permute-start.8 = (f32[128,256]{1,0:T(8,128)S(1)}, f32[128,256]{1,0:T(8,128)S(1)}, u32[]{:S(2)}, u32[]{:S(2)}) collective-permute-start(f32[128,256]{1,0:T(8,128)S(1)} %get-tuple-element.48), channel_id=1, source_target_pairs={{0,2},{1,3},{2,0},{3,1},{4,6},{5,7},{6,4},{7,5},{8,10},{9,11},{10,... | collective-permute-start | bytes 393224 | tf_op jit(solution)/shard_map/ppermute | solution.py:347
  32.2 7.2 %collective-permute-start.2 = (f32[72,256]{1,0:T(8,128)S(1)}, f32[72,256]{1,0:T(8,128)S(1)}, u32[]{:S(2)}, u32[]{:S(2)}) collective-permute-start(f32[72,256]{1,0:T(8,128)S(1)} %get-tuple-element.38), channel_id=1, source_target_pairs={{0,4},{1,5},{2,6},{3,7},{4,0},{5,1},{6,2},{7,3},{8,12},{9,13},{10,... | collective-permute-start | bytes 221192 | tf_op jit(solution)/shard_map/ppermute | solution.py:347
  35.8 7.1 %collective-permute-start.9 = (f32[64,256]{1,0:T(8,128)S(1)}, f32[64,256]{1,0:T(8,128)S(1)}, u32[]{:S(2)}, u32[]{:S(2)}) collective-permute-start(f32[64,256]{1,0:T(8,128)S(1)} %get-tuple-element.51), channel_id=1, source_target_pairs={{0,4},{1,5},{2,6},{3,7},{4,0},{5,1},{6,2},{7,3},{8,12},{9,13},{10,... | collective-permute-start | bytes 196616 | tf_op jit(solution)/shard_map/ppermute | solution.py:347
  39.0 5.9 %collective-permute-start.11 = (f32[64,256]{1,0:T(8,128)S(1)}, f32[64,256]{1,0:T(8,128)S(1)}, u32[]{:S(2)}, u32[]{:S(2)}) collective-permute-start(f32[64,256]{1,0:T(8,128)S(1)} %get-tuple-element.55), channel_id=1, source_target_pairs={{0,4},{1,5},{2,6},{3,7},{4,0},{5,1},{6,2},{7,3},{8,12},{9,13},{10,... | collective-permute-start | bytes 196616 | tf_op jit(solution)/shard_map/ppermute | solution.py:347
  39.6 5.4 %collective-permute-start.5 = (f32[8,128]{1,0:T(8,128)S(1)}, f32[8,128]{1,0:T(8,128)S(1)}, u32[]{:S(2)}, u32[]{:S(2)}) collective-permute-start(f32[8,128]{1,0:T(8,128)S(1)} %shard_map.72.refs_0_), channel_id=1, source_target_pairs={{0,24},{8,16},{16,8},{24,0},{1,25},{9,17},{17,9},{25,1},{2,26},{10... | collective-permute-start | bytes 12296 | tf_op jit(solution)/shard_map/ppermute | solution.py:382
  39.6 5.3 %collective-permute-start.4 = (f32[8,128]{1,0:T(8,128)S(1)}, f32[8,128]{1,0:T(8,128)S(1)}, u32[]{:S(2)}, u32[]{:S(2)}) collective-permute-start(f32[8,128]{1,0:T(8,128)S(1)} %shard_map.72.refs_0_), channel_id=1, source_target_pairs={{0,16},{8,24},{16,0},{24,8},{1,17},{9,25},{17,1},{25,9},{2,18},{10... | collective-permute-start | bytes 12296 | tf_op jit(solution)/shard_map/ppermute | solution.py:382
  41.2 3.8 %collective-permute-start.3 = (f32[8,128]{1,0:T(8,128)S(1)}, f32[8,128]{1,0:T(8,128)S(1)}, u32[]{:S(2)}, u32[]{:S(2)}) collective-permute-start(f32[8,128]{1,0:T(8,128)S(1)} %shard_map.72.refs_0_), channel_id=1, source_target_pairs={{0,8},{8,0},{16,24},{24,16},{1,9},{9,1},{17,25},{25,17},{2,10},{10... | collective-permute-start | bytes 12296 | tf_op jit(solution)/shard_map/ppermute | solution.py:382
